TPU v7x, 32 devices: a whole 2x2x4 slice. The times are simulated.
32 devices in a mesh: beam: 2 (over y), chan: 4 (over z), tgrp: 2 (over x), pol: 2 (over core).
Axes of the slice: x: 2, y: 2, z: 4, core: 2. Of those that a mesh axis runs over, the one named last changes fastest.
Arguments:
- voltages: bfloat16 [16, 8192, 512], P(('beam', 'chan', 'tgrp'), None, 'pol'), parts along dimension 0, may hold values from -6 to 6
- filter_taps: float32 [4, 8192], replicated, may hold values from -0.03125 to 0.03125
Outputs:
- visibility: float32 [512, 16, 2, 512], P('tgrp', ('beam', 'chan'), None, 'pol'), parts along dimension 1
There are 2 independent parts, one for each index of `beam`. A program takes and returns all parts, laid end to end along the dimension named above; an argument that names none is the same for every part. Nothing has to cross between parts.
All inputs are finite; a program needn't handle non-finite values.
Results may differ from a plain program's by a relative error of at most 0.013.
Values may be sent and summed in bfloat16 or wider, within the bound.
A program may use at most 64 MiB of HBM per device.

v0:
```python
import math

import jax
import jax.numpy as jnp
from jax import lax
from jax.sharding import PartitionSpec as P

BAND_START = 1024
CH_DEV = 2


def passed_along(array, axis, by):
    peers = lax.axis_size(axis)
    pairs = [(i, i + by) for i in range(peers) if 0 <= i + by < peers]
    return lax.ppermute(array, axis, pairs)


def twiddle_table(length, band):
    sample = lax.broadcasted_iota(jnp.int32, (length, band), 0)
    channel = lax.broadcasted_iota(jnp.int32, (length, band), 1) + BAND_START
    angles = (sample * channel % length).astype(jnp.float32) * (2.0 * math.pi / length)
    return jnp.concatenate([jnp.cos(angles), -jnp.sin(angles)], 1)


def transform(twiddle, frame_data):
    return lax.dot_general(
        twiddle,
        frame_data,
        (((0,), (0,)), ((), ())),
        precision=lax.Precision.HIGHEST,
        preferred_element_type=jnp.float32,
    )


def body(voltages, filter_taps):
    length = voltages.shape[1]
    half_inputs = voltages.shape[2]
    tap_count = filter_taps.shape[0]
    lead_count = tap_count - 1
    band = CH_DEV * lax.axis_size("chan")
    twiddle = twiddle_table(length, band)
    own_frame = voltages[0]
    frame_wide = own_frame.astype(jnp.float32)

    def tap_term(tap_index):
        return transform(twiddle * filter_taps[tap_index][:, None], frame_wide)

    spectra = tap_term(lead_count)
    for shift_by in range(1, tap_count):
        spectra = spectra + passed_along(
            tap_term(lead_count - shift_by), ("chan", "tgrp"), shift_by
        )
    spectra = spectra.astype(jnp.bfloat16).reshape(1, 2, band, half_inputs)
    turned = lax.all_to_all(spectra, "chan", split_axis=2, concat_axis=0, tiled=True)
    gathered = lax.all_gather(turned, "pol", axis=3, tiled=True)
    inverse_count = 1.0 / (lax.axis_size("chan") * lax.axis_size("tgrp"))
    swapped = jnp.stack([gathered[:, 1], -gathered[:, 0]], 1)
    stacked = jnp.stack([gathered, swapped], 1)
    return lax.psum_scatter(
        (
            jnp.einsum("fopkc,fpkj->ckoj", stacked, turned, preferred_element_type=jnp.float32)
            * inverse_count
        ).astype(jnp.bfloat16),
        "tgrp",
        scatter_dimension=0,
        tiled=True,
    ).astype(jnp.float32)


def solution(mesh):
    return jax.shard_map(
        body,
        mesh=mesh,
        in_specs=(P(("beam", "chan", "tgrp"), None, "pol"), P()),
        out_specs=P("tgrp", ("beam", "chan"), None, "pol"),
        check_vma=False,
    )
```

profile of v0, /device:TPU:0, one launch (start us, length us, event | category | flops | bytes accessed | tf_op | source)
XLA Modules:
  0.0 72.8 jit_solution(17873396575523659024)
XLA Ops:
  6.5 0.0 reduce-scatter.2.cloned.1.call-start
  6.5 0.0 copy-start
  6.5 1.4 %fusion.50 = (f32[1,8192]{1,0:T(1,128)S(1)}, f32[1,8192]{1,0:T(1,128)S(1)}, f32[1,8192]{1,0:T(1,128)S(1)}, f32[1,8192]{1,0:T(1,128)S(1)}) fusion(f32[4,8192]{1,0:T(4,128)} %param.3), kind=kLoop, calls=%fused_computation.50 | loop fusion | bytes 262144 | tf_op jit(solution)/shard_map/slice | solution.py:46
  7.9 1.1 %fusion.39 = (f32[8192,8]{0,1:T(8,128)S(1)}, f32[8192,8]{0,1:T(8,128)S(1)}) fusion(s32[8]{0:T(128)S(1)} %iota_add_fusion), kind=kLoop, calls=%fused_computation.35 | loop fusion | flops 983040 | bytes 524320 | tf_op jit(solution)/shard_map/cos | solution.py:22
  9.0 4.0 %fusion = f32[16,256]{1,0:T(8,128)S(1)} fusion(bf16[1,8192,256]{2,1,0:T(8,128)(2,1)} %param.2, f32[8192]{0:T(1024)S(1)} %bitcast.55, f32[8192,8]{0,1:T(8,128)S(1)} %get-tuple-element.12, f32[8192,8]{0,1:T(8,128)S(1)} %get-tuple-element.11), kind=kOutput, calls=%fused_computation | convolution fusion | flops 402915328 | bytes 4767744 | tf_op jit(solution)/shard_map/dot_general | solution.py:26
  13.0 5.9 %collective-permute-start.2 = (f32[16,256]{1,0:T(8,128)S(1)}, f32[16,256]{1,0:T(8,128)S(1)}, u32[]{:S(2)}, u32[]{:S(2)}) collective-permute-start(f32[16,256]{1,0:T(8,128)S(1)} %fusion), channel_id=1, source_target_pairs={{0,6},{2,8},{4,10},{6,12},{8,14},{1,7},{3,9},{5,11},{7,13},{9,15},... | collective-permute-start | bytes 49160 | tf_op jit(solution)/shard_map/ppermute | solution.py:15
  18.9 0.0 copy-done
  18.9 1.8 %fusion.2 = f32[16,256]{1,0:T(8,128)S(1)} fusion(bf16[1,8192,256]{2,1,0:T(8,128)(2,1)S(1)} %copy-done, f32[8192]{0:T(1024)S(1)} %bitcast.54, f32[8192,8]{0,1:T(8,128)S(1)} %get-tuple-element.12, f32[8192,8]{0,1:T(8,128)S(1)} %get-tuple-element.11), kind=kOutput, calls=%fused_computation.2 | convolution fusion | flops 402915328 | bytes 4767744 | tf_op jit(solution)/shard_map/dot_general | solution.py:26
  20.7 3.5 %collective-permute-start.1 = (f32[16,256]{1,0:T(8,128)S(1)}, f32[16,256]{1,0:T(8,128)S(1)}, u32[]{:S(2)}, u32[]{:S(2)}) collective-permute-start(f32[16,256]{1,0:T(8,128)S(1)} %fusion.2), channel_id=1, source_target_pairs={{0,4},{2,6},{4,8},{6,10},{8,12},{10,14},{1,5},{3,7},{5,9},{7,11},{... | collective-permute-start | bytes 49160 | tf_op jit(solution)/shard_map/ppermute | solution.py:15
  24.2 1.8 %fusion.4 = f32[16,256]{1,0:T(8,128)S(1)} fusion(bf16[1,8192,256]{2,1,0:T(8,128)(2,1)S(1)} %copy-done, f32[8192]{0:T(1024)S(1)} %bitcast.53, f32[8192,8]{0,1:T(8,128)S(1)} %get-tuple-element.12, f32[8192,8]{0,1:T(8,128)S(1)} %get-tuple-element.11), kind=kOutput, calls=%fused_computation.4 | convolution fusion | flops 402915328 | bytes 4767744 | tf_op jit(solution)/shard_map/dot_general | solution.py:26
  26.0 3.5 %collective-permute-start = (f32[16,256]{1,0:T(8,128)S(1)}, f32[16,256]{1,0:T(8,128)S(1)}, u32[]{:S(2)}, u32[]{:S(2)}) collective-permute-start(f32[16,256]{1,0:T(8,128)S(1)} %fusion.4), channel_id=1, source_target_pairs={{0,2},{2,4},{4,6},{6,8},{8,10},{10,12},{12,14},{1,3},{3,5},{5,7},{... | collective-permute-start | bytes 49160 | tf_op jit(solution)/shard_map/ppermute | solution.py:15
  29.4 0.0 collective-permute-done.2
  29.4 0.0 collective-permute-done.1
  29.5 1.4 %collective-permute-done = f32[16,256]{1,0:T(8,128)S(1)} collective-permute-done((f32[16,256]{1,0:T(8,128)S(1)}, f32[16,256]{1,0:T(8,128)S(1)}, u32[]{:S(2)}, u32[]{:S(2)}) %collective-permute-start) | collective-permute-done | bytes 16416 | tf_op jit(solution)/shard_map/ppermute | solution.py:15
  30.9 1.8 %fusion.22 = bf16[1,2,8,256]{3,2,1,0:T(8,128)(2,1)S(1)} fusion(f32[16,256]{1,0:T(8,128)S(1)} %collective-permute-done.2, f32[16,256]{1,0:T(8,128)S(1)} %collective-permute-done.1, f32[16,256]{1,0:T(8,128)S(1)} %collective-permute-done, bf16[1,8192,256]{2,1,0:T(8,128)(2,1)S(1)} %copy-done, f32[8192]{0:T(1024)S(1)} %bitcast.52, ...), kind=kOutput, calls=%fused_computation.15 | convolution fusion | flops 402931712 | bytes 4808704 | tf_op jit(solution)/shard_map/dot_general | solution.py:26
  32.7 9.9 %all_to_all.18 = bf16[1,2,8,256]{3,1,0,2:T(2,128)(2,1)S(1)} all-to-all(bf16[1,2,8,256]{3,1,0,2:T(2,128)(2,1)S(1)} %copy.9), channel_id=1, replica_groups=mesh['beam'=2,'chan'=4,'tgrp'=2,'pol'=2] {'chan'}, dimensions={2} | all-to-all | bytes 16384 | tf_op jit(solution)/shard_map/all_to_all | solution.py:54
  42.6 1.8 %all-gather = bf16[4,1,2,2,512]{4,2,0,3,1:T(2,128)(2,1)S(1)} all-gather(bf16[4,1,2,2,256]{4,2,0,3,1:T(2,128)(2,1)S(1)} %bitcast.56), channel_id=2, replica_groups=mesh['beam'=2,'chan'=4,'tgrp'=2,'pol'=2] {'pol'}, dimensions={4}, use_global_device_ids=true | all-gather | bytes 24576 | tf_op jit(solution)/shard_map/all_gather | solution.py:55
  44.5 1.5 %fusion.9 = bf16[512,2,2,256]{0,3,2,1:T(8,128)(2,1)} fusion(bf16[4,1,2,2,512]{4,2,0,1,3:T(2,128)(2,1)S(1)} %maximum_bitcast_fusion, bf16[4,1,2,2,512]{4,2,0,1,3:T(2,128)(2,1)S(1)} %bitcast.51, bf16[1,2,4,2,256]{4,1,3,2,0:T(2,128)(2,1)S(1)} %bitcast.58), kind=kOutput, calls=%fused_computation.10 | convolution fusion | flops 9502720 | bytes 1089536 | tf_op jit(solution)/shard_map/fopkc,fpkj->ckoj/dot_general | solution.py:61
  46.0 0.0 reduce-scatter.2.cloned.1.call-update
  46.0 17.9 %reduce-scatter.2.cloned.1.call-done = bf16[256,2,2,256]{0,3,2,1:T(8,128)(2,1)} async-done(((bf16[512,2,2,256]{0,3,2,1:T(8,128)(2,1)}), bf16[256,2,2,256]{0,3,2,1:T(8,128)(2,1)}) %reduce-scatter.2.cloned.1.call-update) | async-done | bytes 524304 | tf_op jit(solution)/shard_map/reduce_scatter | solution.py:59
  63.9 2.1 %copy.12 = f32[256,2,2,256]{3,2,1,0:T(2,128)} copy(bf16[256,2,2,256]{0,3,2,1:T(8,128)(2,1)} %reduce-scatter.2.cloned.1.call-done) | data formatting | bytes 1572864 | tf_op jit(solution)/shard_map/convert_element_type | solution.py:67
  (5 shorter events, 0.1 us)
Async XLA Ops:
  6.5 57.3 %reduce-scatter.2.cloned.1.call-start = ((), (), s32[]{:S(2)}) async-start(), calls=%async_computation.2 | async-start | bytes 1572864 | tf_op jit(solution)/shard_map/reduce_scatter | solution.py:59
  6.5 12.4 %copy-start = (bf16[1,8192,256]{2,1,0:T(8,128)(2,1)S(1)}, bf16[1,8192,256]{2,1,0:T(8,128)(2,1)}, u32[]{:S(2)}) copy-start(bf16[1,8192,256]{2,1,0:T(8,128)(2,1)} %param.2) | copy-start | bytes 12582916
  13.0 16.4 %collective-permute-start.2 = (f32[16,256]{1,0:T(8,128)S(1)}, f32[16,256]{1,0:T(8,128)S(1)}, u32[]{:S(2)}, u32[]{:S(2)}) collective-permute-start(f32[16,256]{1,0:T(8,128)S(1)} %fusion), channel_id=1, source_target_pairs={{0,6},{2,8},{4,10},{6,12},{8,14},{1,7},{3,9},{5,11},{7,13},{9,15},... | collective-permute-start | bytes 49160 | tf_op jit(solution)/shard_map/ppermute | solution.py:15
  20.7 8.7 %collective-permute-start.1 = (f32[16,256]{1,0:T(8,128)S(1)}, f32[16,256]{1,0:T(8,128)S(1)}, u32[]{:S(2)}, u32[]{:S(2)}) collective-permute-start(f32[16,256]{1,0:T(8,128)S(1)} %fusion.2), channel_id=1, source_target_pairs={{0,4},{2,6},{4,8},{6,10},{8,12},{10,14},{1,5},{3,7},{5,9},{7,11},{... | collective-permute-start | bytes 49160 | tf_op jit(solution)/shard_map/ppermute | solution.py:15
  26.0 4.9 %collective-permute-start = (f32[16,256]{1,0:T(8,128)S(1)}, f32[16,256]{1,0:T(8,128)S(1)}, u32[]{:S(2)}, u32[]{:S(2)}) collective-permute-start(f32[16,256]{1,0:T(8,128)S(1)} %fusion.4), channel_id=1, source_target_pairs={{0,2},{2,4},{4,6},{6,8},{8,10},{10,12},{12,14},{1,3},{3,5},{5,7},{... | collective-permute-start | bytes 49160 | tf_op jit(solution)/shard_map/ppermute | solution.py:15
Sparse Core Ops, SparseCore 0:
  46.1 17.7 reduce-scatter.1
where the time goes:
time: 73 us; the launch traced here: 72.8 us
  waiting for transfers between devices  19.3 us (26%)
  between operations  13.5 us (18%)
  starting transfers between devices  12.8 us (18%)
  blocking collectives  11.7 us (16%)
  matrix products  10.8 us (15%)
  local copies, waits for them, and re-layouts  3.45 us (5%)
  other arithmetic  1.2 us (2%)
    reduce_scatter x1, waiting for transfers between devices, body(): lax.psum_scatter((jnp.einsum('fopkc,fpkj->ckoj', stacked, turned, preferr...  17.9 us
    ppermute x3, starting transfers between devices, passed_along(): return lax.ppermute(array, axis, pairs)  12.8 us
    all_to_all x1, blocking collectives, body(): lax.all_to_all(spectra, 'chan', split_axis=2, concat_axis=0, tiled=True)  9.89 us
    dot_general x4, matrix products, transform(): lax.dot_general(twiddle, frame_data, (((0,), (0,)), ((), ())), precision=...  9.35 us
    convert_element_type x1, local copies, waits for them, and re-layouts, body(): return lax.psum_scatter((jnp.einsum('fopkc,fpkj->ckoj', stacked, turned,...  2.05 us
    all_gather x1, blocking collectives, body(): gathered = lax.all_gather(turned, 'pol', axis=3, tiled=True)  1.82 us
    dot_general x1, matrix products, body(): jnp.einsum('fopkc,fpkj->ckoj', stacked, turned, preferred_element_type=jn...  1.48 us
  transfers between devices with their start and end apart: 4, of which 2 were waited for; matrix products, arithmetic and copies ran while one was open for 5% of the time, Pallas kernels for 0%

commit v1 on v0

v1 whole, which is shorter than its diff:
```python
import functools
import math

import jax
import jax.numpy as jnp
import numpy as np
from jax import lax
from jax.experimental import pallas as pl
from jax.experimental.pallas import tpu as pltpu
from jax.sharding import PartitionSpec as P

BAND_START = 1024
CH_DEV = 2
CHUNKS = 8
FUSED = False
LINK = jnp.bfloat16
MESH = pl.DeviceIdType.MESH


def twiddle_table(length, chans):
    block, part, sub = np.meshgrid(np.arange(chans), np.arange(2), np.arange(CH_DEV), indexing="ij")
    channel = (BAND_START + block * CH_DEV + sub).reshape(-1, 1)
    angles = (channel * np.arange(length)[None] % length) * (2.0 * math.pi / length)
    return np.where(part.reshape(-1, 1) == 0, np.cos(angles), -np.sin(angles)).astype(np.float32)


def tap_sum_matrix(frames, taps, swapped):
    rows, cols = CH_DEV * frames * 2, frames * taps * 2 * CH_DEV
    row = lax.broadcasted_iota(jnp.int32, (rows, cols), 0)
    col = lax.broadcasted_iota(jnp.int32, (rows, cols), 1)
    row_sub, row_frame, row_part = row // (2 * frames), row // 2 % frames, row % 2
    col_frame, col_tap = col // (taps * 2 * CH_DEV), col // (2 * CH_DEV) % taps
    col_part, col_sub = col // CH_DEV % 2, col % CH_DEV
    hit = (row_sub == col_sub) & (row_frame == col_frame + (taps - 1) - col_tap)
    if swapped:
        hit = hit & (row_part != col_part)
        value = jnp.where(row_part == 0, 1.0, -1.0)
    else:
        hit = hit & (row_part == col_part)
        value = jnp.float32(1.0)
    return jnp.where(hit, value, 0.0).astype(jnp.bfloat16)


def tap_summed(matrix, slots):
    flat = slots.reshape(slots.shape[0] * slots.shape[1], slots.shape[2])
    high = flat.astype(jnp.bfloat16)
    total = jnp.dot(matrix, high, preferred_element_type=jnp.float32)
    if flat.dtype == jnp.float32:
        low = (flat - high.astype(jnp.float32)).astype(jnp.bfloat16)
        total = total + jnp.dot(matrix, low, preferred_element_type=jnp.float32)
    return total.astype(jnp.bfloat16)


def cross_powers(out_ref, wide_ref, row_side, col_side, frames):
    half = col_side.shape[1]
    rows = out_ref.shape[0] * 128 // (CH_DEV * 2 * half)
    tiles = half // 128
    stride = CH_DEV * 2 * tiles
    for part in range(2):
        for sub in range(CH_DEV):
            span = slice(sub * 2 * frames, (sub + 1) * 2 * frames)
            vis = lax.dot_general(
                row_side[part][span],
                col_side[span],
                (((0,), (0,)), ((), ())),
                preferred_element_type=jnp.float32,
            ) * (1.0 / frames)
            if rows != half:
                wide_ref[...] = vis
                first = lax.axis_index("tgrp") * rows % half
                vis = wide_ref[pl.ds(pl.multiple_of(first, 8), rows), :]
            for tile in range(tiles):
                out_ref[pl.ds(sub * 2 * tiles + tile * 2 + part, rows, stride=stride), :] = vis[
                    :, tile * 128 : (tile + 1) * 128
                ]


def exchange_kernel(
    chans, groups, volt_hbm, taps_hbm, tw_hbm, rows_out, cols_out,
    volt, taps, tw, sent, cols, rows, load_sem, col_send, row_send, col_recv, row_recv,
):
    length, half = volt.shape
    tap_count = taps.shape[0]
    frames = chans * groups
    me_c, me_g, me_p = lax.axis_index("chan"), lax.axis_index("tgrp"), lax.axis_index("pol")
    me_f = me_c * groups + me_g
    per_half = groups // 2
    my_half = me_g // per_half
    chunk = length // CHUNKS

    loads = [
        pltpu.make_async_copy(taps_hbm, taps, load_sem.at[0]),
        pltpu.make_async_copy(tw_hbm, tw, load_sem.at[1]),
    ]
    for step in range(CHUNKS):
        span = pl.ds(step * chunk, chunk)
        loads.append(pltpu.make_async_copy(volt_hbm.at[0, span], volt.at[span], load_sem.at[2 + step]))
    for load in loads:
        load.start()

    barrier = pltpu.get_barrier_semaphore()
    for dc in range(chans):
        for dg in range(groups):
            for dp in range(2):
                if dc or dg or dp:
                    peer = {
                        "chan": lax.rem(me_c + dc, chans),
                        "tgrp": lax.rem(me_g + dg, groups),
                        "pol": lax.rem(me_p + dp, 2),
                    }
                    pl.semaphore_signal(barrier, inc=1, device_id=peer, device_id_type=MESH)

    matrix = tap_sum_matrix(frames, tap_count, False)
    swapped = tap_sum_matrix(frames, tap_count, True)

    loads[0].wait()
    loads[1].wait()
    band_rows = tw.shape[0]
    total = jnp.zeros((2 * tap_count * band_rows, half), jnp.float32)
    for step in range(CHUNKS):
        span = slice(step * chunk, (step + 1) * chunk)
        table = tw[:, span]
        wide = jnp.concatenate([table * taps[t : t + 1, span] for t in range(tap_count)], 0)
        high = wide.astype(jnp.bfloat16)
        low = (wide - high.astype(jnp.float32)).astype(jnp.bfloat16)
        loads[2 + step].wait()
        total = total + jnp.dot(
            jnp.concatenate([high, low], 0), volt[span], preferred_element_type=jnp.float32
        )
    terms = total[: tap_count * band_rows] + total[tap_count * band_rows :]
    per_block = 2 * CH_DEV
    for block in range(chans):
        sent[block] = jnp.concatenate(
            [
                terms[t * band_rows + block * per_block : t * band_rows + (block + 1) * per_block]
                for t in range(tap_count)
            ],
            0,
        ).astype(LINK)

    pl.semaphore_wait(barrier, chans * groups * 2 - 1)

    def col_copy(slot, to_c, to_g, index):
        return pltpu.make_async_remote_copy(
            src_ref=sent.at[to_c],
            dst_ref=cols.at[slot],
            send_sem=col_send.at[index],
            recv_sem=col_recv.at[slot],
            device_id={"chan": to_c, "tgrp": to_g, "pol": me_p},
            device_id_type=MESH,
        )

    def row_copy(slot, to_c, to_g, index):
        return pltpu.make_async_remote_copy(
            src_ref=sent.at[to_c],
            dst_ref=rows.at[slot],
            send_sem=row_send.at[index],
            recv_sem=row_recv.at[slot],
            device_id={"chan": to_c, "tgrp": to_g, "pol": 1 - me_p},
            device_id_type=MESH,
        )

    copies = []
    for dc in list(range(1, chans)) + [0]:
        to_c = lax.rem(me_c + dc, chans)
        for dg in range(groups):
            if dc or dg:
                copies.append(col_copy(me_f, to_c, lax.rem(me_g + dg, groups), dc * groups + dg))
                copies[-1].start()
        for member in range(per_half):
            to_g = me_p * per_half + member
            copies.append(row_copy(me_f, to_c, to_g, dc * per_half + member))
            copies[-1].start()
    cols[me_f] = sent[me_c]

    for dc in range(chans):
        for dg in range(groups):
            if dc or dg:
                from_c, from_g = lax.rem(me_c + dc, chans), lax.rem(me_g + dg, groups)
                col_copy(from_c * groups + from_g, me_c, me_g, 0).wait_recv()
    slots = cols[...]
    cols_out[...] = tap_summed(matrix, slots)

    @pl.when(my_half == me_p)
    def _():
        rows_out[0] = cols_out[...]
        rows_out[1] = tap_summed(swapped, slots)

    @pl.when(my_half != me_p)
    def _():
        for source in range(frames):
            row_copy(source, me_c, me_g, 0).wait_recv()
        far = rows[...]
        rows_out[0] = tap_summed(matrix, far)
        rows_out[1] = tap_summed(swapped, far)

    for copy in copies:
        copy.wait_send()


def power_kernel(frames, row_side, col_side, out_ref, *wide):
    cross_powers(out_ref, wide[0] if wide else None, row_side[...], col_side[...], frames)


def body(voltages, filter_taps):
    chans, groups = lax.axis_size("chan"), lax.axis_size("tgrp")
    _, length, half = voltages.shape
    taps = filter_taps.shape[0]
    frames = chans * groups
    slot = taps * 2 * CH_DEV
    table = jnp.asarray(twiddle_table(length, chans))
    vmem = pl.BlockSpec(memory_space=pltpu.VMEM)
    summed = CH_DEV * 2 * frames
    row_side, col_side = pl.pallas_call(
        functools.partial(exchange_kernel, chans, groups),
        out_shape=(
            jax.ShapeDtypeStruct((2, summed, half), jnp.bfloat16),
            jax.ShapeDtypeStruct((summed, half), jnp.bfloat16),
        ),
        in_specs=[pl.BlockSpec(memory_space=pl.ANY)] * 3,
        out_specs=(vmem, vmem),
        scratch_shapes=[
            pltpu.VMEM((length, half), jnp.bfloat16),
            pltpu.VMEM(filter_taps.shape, jnp.float32),
            pltpu.VMEM(table.shape, jnp.float32),
            pltpu.VMEM((chans, slot, half), LINK),
            pltpu.VMEM((frames, slot, half), LINK),
            pltpu.VMEM((frames, slot, half), LINK),
            pltpu.SemaphoreType.DMA((2 + CHUNKS,)),
            pltpu.SemaphoreType.DMA((frames,)),
            pltpu.SemaphoreType.DMA((frames // 2,)),
            pltpu.SemaphoreType.DMA((frames,)),
            pltpu.SemaphoreType.DMA((frames,)),
        ],
        compiler_params=pltpu.CompilerParams(collective_id=0, has_side_effects=True),
        name="exchange",
    )(voltages, filter_taps, table)
    rows = half * lax.axis_size("pol") // groups
    tiles = half // 128
    powers = pl.pallas_call(
        functools.partial(power_kernel, frames),
        out_shape=jax.ShapeDtypeStruct((rows * CH_DEV * tiles * 2, 128), jnp.float32),
        in_specs=[vmem, vmem],
        out_specs=vmem,
        scratch_shapes=[] if rows == half else [pltpu.VMEM((half, half), jnp.float32)],
        name="powers",
    )(row_side, col_side)
    powers = powers.reshape(rows, CH_DEV, tiles, 2, 128).transpose(0, 1, 3, 2, 4)
    return powers.reshape(rows, CH_DEV, 2, half)


def solution(mesh):
    return jax.shard_map(
        body,
        mesh=mesh,
        in_specs=(P(("beam", "chan", "tgrp"), None, "pol"), P()),
        out_specs=P("tgrp", ("beam", "chan"), None, "pol"),
        check_vma=False,
    )
```

time: 73 us -> 14.2 us (0.19)
  waiting for transfers between devices: 19.3 us -> 0 us
  Pallas kernels: 0 us -> 14.1 us
  between operations: 13.5 us -> 0.01 us
  starting transfers between devices: 12.8 us -> 0 us
  blocking collectives: 11.7 us -> 0 us
  matrix products: 10.8 us -> 0 us
  local copies, waits for them, and re-layouts: 3.45 us -> 0 us
  other arithmetic: 1.2 us -> 0 us
    reduce_scatter x1 -> x0, waiting for transfers between devices: 17.9 us -> none  [body(): lax.psum_scatter((jnp.einsum('fopkc,fpkj->ckoj', stacked, turned, preferr...]
    pallas_call x0 -> x2, Pallas kernels: none -> 14.1 us  [the longest x1 11.9 us: body(): pl.pallas_call(functools.partial(exchange_kernel, chans, groups), out_sha...]
    ppermute x3 -> x0, starting transfers between devices: 12.8 us -> none  [passed_along(): return lax.ppermute(array, axis, pairs)]
    dot_general x5 -> x0, matrix products: 10.8 us -> none  [the longest x4 9.35 us: transform(): lax.dot_general(twiddle, frame_data, (((0,), (0,)), ((), ())), precision=...]
    all_to_all x1 -> x0, blocking collectives: 9.89 us -> none  [body(): lax.all_to_all(spectra, 'chan', split_axis=2, concat_axis=0, tiled=True)]
    convert_element_type x1 -> x0, local copies, waits for them, and re-layouts: 2.05 us -> none  [body(): return lax.psum_scatter((jnp.einsum('fopkc,fpkj->ckoj', stacked, turned,...]
    all_gather x1 -> x0, blocking collectives: 1.82 us -> none  [body(): gathered = lax.all_gather(turned, 'pol', axis=3, tiled=True)]
    ppermute x3 -> x0, waiting for transfers between devices: 1.41 us -> none  [passed_along(): return lax.ppermute(array, axis, pairs)]
  transfers between devices with their start and end apart: 4 -> 0, of which waited for: 2 -> 0; matrix products, arithmetic and copies ran while one was open for 5% -> 0% of each run, Pallas kernels for 0% -> 0%
where the time goes in v1:
time: 14.2 us; the launch traced here: 14.1 us
  Pallas kernels  14.1 us (99%)
    pallas_call x1, Pallas kernels, body(): pl.pallas_call(functools.partial(exchange_kernel, chans, groups), out_sha...  11.9 us
    pallas_call x1, Pallas kernels, body(): pl.pallas_call(functools.partial(power_kernel, frames), out_shape=jax.Sha...  2.1 us

profile of v1, /device:TPU:0, one launch (start us, length us, event | category | flops | bytes accessed | tf_op | source)
XLA Modules:
  0.0 14.1 jit_solution(5471265877335948761)
XLA Ops:
  0.0 11.9 %exchange.1 = (bf16[2,32,256]{2,1,0:T(8,128)(2,1)}, bf16[32,256]{1,0:T(8,128)(2,1)}) custom-call(bf16[1,8192,256]{2,1,0:T(8,128)(2,1)} %volt_hbm.1, f32[4,8192]{1,0:T(4,128)} %taps_hbm.1, f32[16,8192]{1,0:T(8,128)} %constant.2.clone.tw_hbm), custom_call_target="tpu_custom_call" | custom-call | tf_op jit(solution)/shard_map/exchange/pallas_call | solution.py:214
  12.0 2.1 %powers.1 = f32[2048,128]{1,0:T(8,128)} custom-call(bf16[2,32,256]{2,1,0:T(8,128)(2,1)} %get-tuple-element.7.row_side, bf16[32,256]{1,0:T(8,128)(2,1)} %get-tuple-element.8.col_side), custom_call_target="tpu_custom_call" | custom-call | tf_op jit(solution)/shard_map/powers/pallas_call | solution.py:240

commit v2 on v1

--- a/solution.py
+++ b/solution.py
@@ -12,7 +12,8 @@
 BAND_START = 1024
 CH_DEV = 2
 CHUNKS = 8
-FUSED = False
+VMEM_BYTES = 64 * 2**20
+SPARE_BYTES = 72 * 2**10
 LINK = jnp.bfloat16
 MESH = pl.DeviceIdType.MESH
 
@@ -21,7 +22,15 @@
     block, part, sub = np.meshgrid(np.arange(chans), np.arange(2), np.arange(CH_DEV), indexing="ij")
     channel = (BAND_START + block * CH_DEV + sub).reshape(-1, 1)
     angles = (channel * np.arange(length)[None] % length) * (2.0 * math.pi / length)
-    return np.where(part.reshape(-1, 1) == 0, np.cos(angles), -np.sin(angles)).astype(np.float32)
+    is_real = part.reshape(-1, 1) == 0
+    chunk = length // CHUNKS
+    near, turn = angles[:, :chunk], angles[:, ::chunk]
+    table = np.zeros((2 * len(angles), chunk + 128), np.float32)
+    table[: len(angles), :chunk] = np.where(is_real, np.cos(near), -np.sin(near))
+    table[len(angles) :, :chunk] = np.where(is_real, -np.sin(near), np.cos(near))
+    table[: len(angles), chunk : chunk + CHUNKS] = np.cos(turn)
+    table[len(angles) :, chunk : chunk + CHUNKS] = np.where(is_real, np.sin(turn), -np.sin(turn))
+    return table
 
 
 def tap_sum_matrix(frames, taps, swapped):
@@ -51,28 +60,37 @@
     return total.astype(jnp.bfloat16)
 
 
-def cross_powers(out_ref, wide_ref, row_side, col_side, frames):
+def power_kernel(frames, row_side, col_side, out_hbm, out_ref, wide_ref, sems):
     half = col_side.shape[1]
     rows = out_ref.shape[0] * 128 // (CH_DEV * 2 * half)
     tiles = half // 128
     stride = CH_DEV * 2 * tiles
-    for part in range(2):
-        for sub in range(CH_DEV):
-            span = slice(sub * 2 * frames, (sub + 1) * 2 * frames)
-            vis = lax.dot_general(
-                row_side[part][span],
-                col_side[span],
-                (((0,), (0,)), ((), ())),
-                preferred_element_type=jnp.float32,
-            ) * (1.0 / frames)
-            if rows != half:
-                wide_ref[...] = vis
-                first = lax.axis_index("tgrp") * rows % half
-                vis = wide_ref[pl.ds(pl.multiple_of(first, 8), rows), :]
-            for tile in range(tiles):
-                out_ref[pl.ds(sub * 2 * tiles + tile * 2 + part, rows, stride=stride), :] = vis[
-                    :, tile * 128 : (tile + 1) * 128
-                ]
+    pieces = rows // 128 if rows == half else 1
+    size = rows // pieces
+    writes = []
+    for piece in range(pieces):
+        for part in range(2):
+            for sub in range(CH_DEV):
+                span = slice(sub * 2 * frames, (sub + 1) * 2 * frames)
+                lanes = slice(piece * size, (piece + 1) * size) if rows == half else slice(None)
+                vis = lax.dot_general(
+                    row_side[part, span, lanes],
+                    col_side[span],
+                    (((0,), (0,)), ((), ())),
+                    preferred_element_type=jnp.float32,
+                ) * (1.0 / frames)
+                if rows != half:
+                    wide_ref[...] = vis
+                    first = lax.axis_index("tgrp") * rows % half
+                    vis = wide_ref[pl.ds(pl.multiple_of(first, 8), rows), :]
+                for tile in range(tiles):
+                    start = piece * size * stride + sub * 2 * tiles + tile * 2 + part
+                    out_ref[pl.ds(start, size, stride=stride), :] = vis[:, tile * 128 : (tile + 1) * 128]
+        region = pl.ds(piece * size * stride, size * stride)
+        writes.append(pltpu.make_async_copy(out_ref.at[region], out_hbm.at[region], sems.at[piece]))
+        writes[-1].start()
+    for write in writes:
+        write.wait()
 
 
 def exchange_kernel(
@@ -115,11 +133,13 @@
 
     loads[0].wait()
     loads[1].wait()
-    band_rows = tw.shape[0]
+    band_rows = tw.shape[0] // 2
+    own, other = tw[:band_rows, :chunk], tw[band_rows:, :chunk]
     total = jnp.zeros((2 * tap_count * band_rows, half), jnp.float32)
     for step in range(CHUNKS):
         span = slice(step * chunk, (step + 1) * chunk)
-        table = tw[:, span]
+        column = slice(chunk + step, chunk + step + 1)
+        table = tw[:band_rows, column] * own + tw[band_rows:, column] * other
         wide = jnp.concatenate([table * taps[t : t + 1, span] for t in range(tap_count)], 0)
         high = wide.astype(jnp.bfloat16)
         low = (wide - high.astype(jnp.float32)).astype(jnp.bfloat16)
@@ -160,17 +180,20 @@
             device_id_type=MESH,
         )
 
-    copies = []
-    for dc in list(range(1, chans)) + [0]:
-        to_c = lax.rem(me_c + dc, chans)
-        for dg in range(groups):
-            if dc or dg:
-                copies.append(col_copy(me_f, to_c, lax.rem(me_g + dg, groups), dc * groups + dg))
-                copies[-1].start()
-        for member in range(per_half):
-            to_g = me_p * per_half + member
-            copies.append(row_copy(me_f, to_c, to_g, dc * per_half + member))
-            copies[-1].start()
+    def each_send(act):
+        for place in range(chans):
+            to_c = jnp.where(me_c < chans // 2, chans - 1 - place, place)
+            for dg in reversed(range(groups)):
+                to_g = lax.rem(me_g + dg, groups)
+                copy = col_copy(me_f, to_c, to_g, place * groups + dg)
+                if dg:
+                    act(copy)
+                else:
+                    pl.when(to_c != me_c)(functools.partial(act, copy))
+            for member in range(per_half):
+                act(row_copy(me_f, to_c, me_p * per_half + member, place * per_half + member))
+
+    each_send(lambda copy: copy.start())
     cols[me_f] = sent[me_c]
 
     for dc in range(chans):
@@ -194,12 +217,7 @@
         rows_out[0] = tap_summed(matrix, far)
         rows_out[1] = tap_summed(swapped, far)
 
-    for copy in copies:
-        copy.wait_send()
-
-
-def power_kernel(frames, row_side, col_side, out_ref, *wide):
-    cross_powers(out_ref, wide[0] if wide else None, row_side[...], col_side[...], frames)
+    each_send(lambda copy: copy.wait_send())
 
 
 def body(voltages, filter_taps):
@@ -214,8 +232,8 @@
     row_side, col_side = pl.pallas_call(
         functools.partial(exchange_kernel, chans, groups),
         out_shape=(
-            jax.ShapeDtypeStruct((2, summed, half), jnp.bfloat16),
-            jax.ShapeDtypeStruct((summed, half), jnp.bfloat16),
+            pltpu.VMEM((2, summed, half), jnp.bfloat16),
+            pltpu.VMEM((summed, half), jnp.bfloat16),
         ),
         in_specs=[pl.BlockSpec(memory_space=pl.ANY)] * 3,
         out_specs=(vmem, vmem),
@@ -232,7 +250,7 @@
             pltpu.SemaphoreType.DMA((frames,)),
             pltpu.SemaphoreType.DMA((frames,)),
         ],
-        compiler_params=pltpu.CompilerParams(collective_id=0, has_side_effects=True),
+        compiler_params=pltpu.CompilerParams(collective_id=0, has_side_effects=True, vmem_limit_bytes=VMEM_BYTES - SPARE_BYTES - 6 * summed * half),
         name="exchange",
     )(voltages, filter_taps, table)
     rows = half * lax.axis_size("pol") // groups
@@ -241,8 +259,13 @@
         functools.partial(power_kernel, frames),
         out_shape=jax.ShapeDtypeStruct((rows * CH_DEV * tiles * 2, 128), jnp.float32),
         in_specs=[vmem, vmem],
-        out_specs=vmem,
-        scratch_shapes=[] if rows == half else [pltpu.VMEM((half, half), jnp.float32)],
+        out_specs=pl.BlockSpec(memory_space=pltpu.HBM),
+        scratch_shapes=[
+            pltpu.VMEM((rows * CH_DEV * tiles * 2, 128), jnp.float32),
+            pltpu.VMEM((half, half) if rows != half else (8, 128), jnp.float32),
+            pltpu.SemaphoreType.DMA((max(1, rows // 128),)),
+        ],
+        compiler_params=pltpu.CompilerParams(vmem_limit_bytes=VMEM_BYTES // 4),
         name="powers",
     )(row_side, col_side)
     powers = powers.reshape(rows, CH_DEV, tiles, 2, 128).transpose(0, 1, 3, 2, 4)

time: 14.2 us -> 12.5 us (0.88)
  Pallas kernels: 14.1 us -> 12.3 us
    pallas_call x1, Pallas kernels: 11.9 us -> 11.1 us  [body(): pl.pallas_call(functools.partial(exchange_kernel, chans, groups), out_sha...]
    pallas_call x1, Pallas kernels: 2.1 us -> 1.26 us  [body(): pl.pallas_call(functools.partial(power_kernel, frames), out_shape=jax.Sha...]
where the time goes in v2:
time: 12.5 us; the launch traced here: 12.4 us
  Pallas kernels  12.3 us (98%)
    pallas_call x1, Pallas kernels, body(): pl.pallas_call(functools.partial(exchange_kernel, chans, groups), out_sha...  11.1 us
    pallas_call x1, Pallas kernels, body(): pl.pallas_call(functools.partial(power_kernel, frames), out_shape=jax.Sha...  1.26 us

profile of v2, /device:TPU:0, one launch (start us, length us, event | category | flops | bytes accessed | tf_op | source)
XLA Modules:
  0.0 12.4 jit_solution(3839441732997038897)
XLA Ops:
  0.0 11.1 %exchange.1 = (bf16[2,32,256]{2,1,0:T(8,128)(2,1)S(1)}, bf16[32,256]{1,0:T(8,128)(2,1)S(1)}) custom-call(bf16[1,8192,256]{2,1,0:T(8,128)(2,1)} %volt_hbm.1, f32[4,8192]{1,0:T(4,128)} %taps_hbm.1, f32[32,1152]{1,0:T(8,128)} %constant.2.clone.tw_hbm), custom_call_target="tpu_custom_call" | custom-call | tf_op jit(solution)/shard_map/exchange/pallas_call | solution.py:232
  11.1 1.3 %powers.1 = f32[2048,128]{1,0:T(8,128)} custom-call(bf16[2,32,256]{2,1,0:T(8,128)(2,1)S(1)} %get-tuple-element.7.row_side, bf16[32,256]{1,0:T(8,128)(2,1)S(1)} %get-tuple-element.8.col_side), custom_call_target="tpu_custom_call" | custom-call | tf_op jit(solution)/shard_map/powers/pallas_call | solution.py:258

commit v3 on v2

--- a/solution.py
+++ b/solution.py
@@ -105,6 +105,7 @@
     per_half = groups // 2
     my_half = me_g // per_half
     chunk = length // CHUNKS
+    per_block = 2 * CH_DEV
 
     loads = [
         pltpu.make_async_copy(taps_hbm, taps, load_sem.at[0]),
@@ -129,7 +130,7 @@
                     pl.semaphore_signal(barrier, inc=1, device_id=peer, device_id_type=MESH)
 
     matrix = tap_sum_matrix(frames, tap_count, False)
-    swapped = tap_sum_matrix(frames, tap_count, True)
+    both = jnp.concatenate([matrix, tap_sum_matrix(frames, tap_count, True)], 0)
 
     loads[0].wait()
     loads[1].wait()
@@ -140,7 +141,16 @@
         span = slice(step * chunk, (step + 1) * chunk)
         column = slice(chunk + step, chunk + step + 1)
         table = tw[:band_rows, column] * own + tw[band_rows:, column] * other
-        wide = jnp.concatenate([table * taps[t : t + 1, span] for t in range(tap_count)], 0)
+        gains = jnp.concatenate(
+            [jnp.broadcast_to(taps[t : t + 1, span], (per_block, chunk)) for t in range(tap_count)], 0
+        )
+        wide = jnp.concatenate(
+            [
+                jnp.concatenate([table[b * per_block : (b + 1) * per_block]] * tap_count, 0) * gains
+                for b in range(chans)
+            ],
+            0,
+        )
         high = wide.astype(jnp.bfloat16)
         low = (wide - high.astype(jnp.float32)).astype(jnp.bfloat16)
         loads[2 + step].wait()
@@ -148,15 +158,7 @@
             jnp.concatenate([high, low], 0), volt[span], preferred_element_type=jnp.float32
         )
     terms = total[: tap_count * band_rows] + total[tap_count * band_rows :]
-    per_block = 2 * CH_DEV
-    for block in range(chans):
-        sent[block] = jnp.concatenate(
-            [
-                terms[t * band_rows + block * per_block : t * band_rows + (block + 1) * per_block]
-                for t in range(tap_count)
-            ],
-            0,
-        ).astype(LINK)
+    sent[...] = terms.reshape(sent.shape).astype(LINK)
 
     pl.semaphore_wait(barrier, chans * groups * 2 - 1)
 
@@ -201,21 +203,22 @@
             if dc or dg:
                 from_c, from_g = lax.rem(me_c + dc, chans), lax.rem(me_g + dg, groups)
                 col_copy(from_c * groups + from_g, me_c, me_g, 0).wait_recv()
-    slots = cols[...]
-    cols_out[...] = tap_summed(matrix, slots)
+    def put_rows(summed):
+        rows_out[0] = summed[: matrix.shape[0]]
+        rows_out[1] = summed[matrix.shape[0] :]
 
     @pl.when(my_half == me_p)
     def _():
-        rows_out[0] = cols_out[...]
-        rows_out[1] = tap_summed(swapped, slots)
+        summed = tap_summed(both, cols[...])
+        cols_out[...] = summed[: matrix.shape[0]]
+        put_rows(summed)
 
     @pl.when(my_half != me_p)
     def _():
+        cols_out[...] = tap_summed(matrix, cols[...])
         for source in range(frames):
             row_copy(source, me_c, me_g, 0).wait_recv()
-        far = rows[...]
-        rows_out[0] = tap_summed(matrix, far)
-        rows_out[1] = tap_summed(swapped, far)
+        put_rows(tap_summed(both, rows[...]))
 
     each_send(lambda copy: copy.wait_send())
 

time: 12.5 us -> 12.5 us (level)
  no operation moved by 1% of the time
where the time goes in v3:
time: 12.5 us; the launch traced here: 12.3 us
  Pallas kernels  12.3 us (98%)
    pallas_call x1, Pallas kernels, body(): pl.pallas_call(functools.partial(exchange_kernel, chans, groups), out_sha...  11.1 us
    pallas_call x1, Pallas kernels, body(): pl.pallas_call(functools.partial(power_kernel, frames), out_shape=jax.Sha...  1.26 us

profile of v3, /device:TPU:0, one launch (start us, length us, event | category | flops | bytes accessed | tf_op | source)
XLA Modules:
  0.0 12.3 jit_solution(10925592520545003394)
XLA Ops:
  0.0 11.1 %exchange.1 = (bf16[2,32,256]{2,1,0:T(8,128)(2,1)S(1)}, bf16[32,256]{1,0:T(8,128)(2,1)S(1)}) custom-call(bf16[1,8192,256]{2,1,0:T(8,128)(2,1)} %volt_hbm.1, f32[4,8192]{1,0:T(4,128)} %taps_hbm.1, f32[32,1152]{1,0:T(8,128)} %constant.2.clone.tw_hbm), custom_call_target="tpu_custom_call" | custom-call | tf_op jit(solution)/shard_map/exchange/pallas_call | solution.py:235
  11.1 1.3 %powers.1 = f32[2048,128]{1,0:T(8,128)} custom-call(bf16[2,32,256]{2,1,0:T(8,128)(2,1)S(1)} %get-tuple-element.7.row_side, bf16[32,256]{1,0:T(8,128)(2,1)S(1)} %get-tuple-element.8.col_side), custom_call_target="tpu_custom_call" | custom-call | tf_op jit(solution)/shard_map/powers/pallas_call | solution.py:261

commit v4 on v3

--- a/solution.py
+++ b/solution.py
@@ -65,7 +65,7 @@
     rows = out_ref.shape[0] * 128 // (CH_DEV * 2 * half)
     tiles = half // 128
     stride = CH_DEV * 2 * tiles
-    pieces = rows // 128 if rows == half else 1
+    pieces = rows // 64 if rows == half else 1
     size = rows // pieces
     writes = []
     for piece in range(pieces):
@@ -266,7 +266,7 @@
         scratch_shapes=[
             pltpu.VMEM((rows * CH_DEV * tiles * 2, 128), jnp.float32),
             pltpu.VMEM((half, half) if rows != half else (8, 128), jnp.float32),
-            pltpu.SemaphoreType.DMA((max(1, rows // 128),)),
+            pltpu.SemaphoreType.DMA((max(1, rows // 64),)),
         ],
         compiler_params=pltpu.CompilerParams(vmem_limit_bytes=VMEM_BYTES // 4),
         name="powers",

time: 12.5 us -> 12.5 us (level)
  no operation moved by 1% of the time
where the time goes in v4:
time: 12.5 us; the launch traced here: 12.3 us
  Pallas kernels  12.3 us (98%)
    pallas_call x1, Pallas kernels, body(): pl.pallas_call(functools.partial(exchange_kernel, chans, groups), out_sha...  11.1 us
    pallas_call x1, Pallas kernels, body(): pl.pallas_call(functools.partial(power_kernel, frames), out_shape=jax.Sha...  1.25 us

profile of v4, /device:TPU:0, one launch (start us, length us, event | category | flops | bytes accessed | tf_op | source)
XLA Modules:
  0.0 12.3 jit_solution(7398003473923403343)
XLA Ops:
  0.0 11.1 %exchange.1 = (bf16[2,32,256]{2,1,0:T(8,128)(2,1)S(1)}, bf16[32,256]{1,0:T(8,128)(2,1)S(1)}) custom-call(bf16[1,8192,256]{2,1,0:T(8,128)(2,1)} %volt_hbm.1, f32[4,8192]{1,0:T(4,128)} %taps_hbm.1, f32[32,1152]{1,0:T(8,128)} %constant.2.clone.tw_hbm), custom_call_target="tpu_custom_call" | custom-call | tf_op jit(solution)/shard_map/exchange/pallas_call | solution.py:235
  11.1 1.2 %powers.1 = f32[2048,128]{1,0:T(8,128)} custom-call(bf16[2,32,256]{2,1,0:T(8,128)(2,1)S(1)} %get-tuple-element.7.row_side, bf16[32,256]{1,0:T(8,128)(2,1)S(1)} %get-tuple-element.8.col_side), custom_call_target="tpu_custom_call" | custom-call | tf_op jit(solution)/shard_map/powers/pallas_call | solution.py:261
